TPU v7x, 32 devices: a whole 2x2x4 slice. The times are simulated.
32 devices in a mesh: tm: 4 (over y, core), scen: 8 (over z, x).
Axes of the slice: x: 2, y: 2, z: 4, core: 2. Of those that a mesh axis runs over, the one named last changes fastest.
Arguments:
- prior_dispatch: float32 [600, 8192], P(None, ('tm', 'scen')), may hold values from 0 to 1
- prior_commitment: float32 [600, 8192], P(None, ('tm', 'scen')), may hold values from 0 to 1
- prior_consensus: float32 [600, 32], P(None, 'tm'), may hold values from 0 to 1
- prior_multiplier: float32 [600, 8192], P(None, ('tm', 'scen')), may hold values from -2 to 2
- flow_factors: bfloat16 [2560, 2000], P('scen'), may hold values from -0.25 to 0.25
- unit_buses: int32 [600], replicated, may hold values from 0 to 1999
- wind_buses: int32 [128], replicated, may hold values from 0 to 1999
- wind_output: bfloat16 [128, 8192], P(None, ('tm', 'scen')), may hold values from 0 to 1
- demand: float32 [32], P('tm'), may hold values from 180 to 300
- load_flows: bfloat16 [2560, 32], P('scen', 'tm'), may hold values from -6 to 6
- line_limits: bfloat16 [2560], P('scen'), may hold values from 0.29882812 to 3
- unit_table: float32 [5, 600], replicated, may hold values from 0.05 to 2, as said below
Outputs:
- dispatch: float32 [600, 8192], P(None, ('tm', 'scen'))
- commitment: float32 [600, 8192], P(None, ('tm', 'scen'))
- consensus: float32 [600, 32], P(None, 'tm')
- multiplier: float32 [600, 8192], P(None, ('tm', 'scen'))
Inputs may be any that keep to these rules, and one draw needn't show every extreme that they name: `unit_table`: rows 0 and 4 lie in 0.1 to 1, row 1 in 0.05 to 0.5, row 2 in 0.5 to 2, row 3 in 0.05 to 0.5.
All inputs are finite; a program needn't handle non-finite values.
Results may differ from a plain program's by a relative error of at most 0.0017.
Values may be sent and summed in bfloat16 or wider, within the bound.
A program may use at most 64 MiB of HBM per device.

v0:
```python
import functools

import jax
import jax.numpy as jnp
from jax import lax
from jax.experimental import pallas as pl
from jax.experimental.pallas import tpu as pltpu
from jax.sharding import PartitionSpec as P

PASSES = 3
H_DEV = 8
MESH = pl.DeviceIdType.MESH

flow_weight = 0.5
ramp_weight = 1.0
balance_weight = 0.004
short_weight = 2.0
penalty = 1.0
step_power = 0.2
step_commit = 0.3


def split(value):
    high = value.astype(jnp.bfloat16)
    rest = value - high.astype(jnp.float32)
    middle = rest.astype(jnp.bfloat16)
    return high, middle, (rest - middle.astype(jnp.float32)).astype(jnp.bfloat16)


def kernel(n_tm, n_scen, units, sel_ref, tab_ref, pd_ref, pc_ref, cons_ref, mu_ref, wind_ref, table_ref, need_ref,
           power_out, commit_out, cons_out,
           fac, fact, load, bound, exc, pw, cm, mult, target, ext, backs, bef, aft,
           tabs, esend, erecv, psend, precv, total_row, small, ut_ref,
           recv_sem, send_sem, tsend, trecv, esem_s, esem_r, psem_s, psem_r):
    rows = sel_ref.shape[0]
    quarter = rows // 4
    up = pw.shape[0]
    cols = pw.shape[1]
    block = cols // H_DEV
    chunk = 2 * rows
    n_z = n_scen // 2
    f32, bf16 = jnp.float32, jnp.bfloat16
    tm = lax.axis_index("tm")
    scen = lax.axis_index("scen")
    y, c = tm // 2, tm % 2
    z, x = scen // 2, scen % 2
    oy = 1 - y
    oc = 1 - c
    ox = 1 - x
    mine = y * 2 + c
    other = oy * 2 + c
    dev_x = (tm, z * 2 + ox)
    dev_y = (oy * 2 + c, scen)
    dev_c = (y * 2 + oc, scen)
    dev_dn = (tm, scen - 2)
    dev_up = (tm, scen + 2)

    def piece(zz, xx, q):
        return (zz * 2 + xx) * 4 + q

    def at(p):
        return fac.at[pl.ds(pl.multiple_of(p * quarter, 16), quarter), :]

    def own(q):
        return sel_ref.at[pl.ds(pl.multiple_of(q * quarter, 16), quarter), :]

    def copy(src, p, slot, dev):
        return pltpu.make_async_remote_copy(
            src_ref=src, dst_ref=at(p), send_sem=send_sem.at[slot, p], recv_sem=recv_sem.at[p],
            device_id=dev, device_id_type=MESH)

    def pass_on(p, slot, dev):
        copy(at(p), p, slot, dev).start()

    def arrived(p):
        copy(at(p), p, 0, dev_x).wait_recv()

    def table_copy(k):
        peer = lax.rem(scen + k, n_scen)
        return pltpu.make_async_remote_copy(
            src_ref=tab_ref, dst_ref=tabs.at[scen], send_sem=tsend.at[k], recv_sem=trecv.at[scen],
            device_id=(tm, peer), device_id_type=MESH)

    barrier = pltpu.get_barrier_semaphore()
    for k in range(1, n_scen):
        pl.semaphore_signal(barrier, inc=1, device_id=(tm, lax.rem(scen + k, n_scen)), device_id_type=MESH)
    for k in range(1, n_tm):
        pl.semaphore_signal(barrier, inc=1, device_id=(lax.rem(tm + k, n_tm), scen), device_id_type=MESH)
    pl.semaphore_wait(barrier, n_scen - 1 + n_tm - 1)

    p_own = piece(z, x, mine)
    p_own2 = piece(z, x, other)

    @pl.when(z > 0)
    def _():
        copy(own(mine), p_own, 0, dev_dn).start()

    @pl.when(z < n_z - 1)
    def _():
        copy(own(mine), p_own, 1, dev_up).start()

    copy(own(mine), p_own, 2, dev_x).start()
    copy(own(other), p_own2, 2, dev_x).start()
    for k in range(1, n_scen):
        table_copy(k).start()

    def edges_of(tile_last, tile_first):
        lane = lax.broadcasted_iota(jnp.int32, (up // 4, 128), 1)
        last = jnp.zeros((up // 4, 128), f32)
        first = jnp.zeros((up // 4, 128), f32)
        for g in range(4):
            inside = (lane >= 32 * g) & (lane < 32 * g + 32)
            a = tile_last[g * (up // 4):(g + 1) * (up // 4), :]
            b = tile_first[g * (up // 4):(g + 1) * (up // 4), :]
            sa = (32 * g - 96) % 128
            sb = (32 * g) % 128
            a = pltpu.roll(a, sa, 1) if sa else a
            b = pltpu.roll(b, sb, 1) if sb else b
            last = jnp.where(inside, a, last)
            first = jnp.where(inside, b, first)
        return last, first

    def edge_copy(number, way):
        dev = (tm + 1, scen) if way == 0 else (tm - 1, scen)
        return pltpu.make_async_remote_copy(
            src_ref=esend.at[number, way], dst_ref=erecv.at[number, way],
            send_sem=esem_s.at[number, way], recv_sem=esem_r.at[number, way],
            device_id=dev, device_id_type=MESH)

    def send_edges(number):
        @pl.when(tm < n_tm - 1)
        def _():
            edge_copy(number, 0).start()

        @pl.when(tm > 0)
        def _():
            edge_copy(number, 1).start()

    def store_edges(number):
        last, first = edges_of(pw[:, cols - 128:], pw[:, :128])
        esend[number, 0] = last
        esend[number, 1] = first

    zero_tail = jnp.zeros((up - units, cols), f32)
    pw[:units, :] = pd_ref[...]
    pw[units:, :] = zero_tail
    store_edges(0)
    cm[:units, :] = pc_ref[...]
    cm[units:, :] = zero_tail
    mult[:units, :] = mu_ref[...]
    mult[units:, :] = zero_tail
    hour_row = lax.broadcasted_iota(jnp.int32, (H_DEV, cols), 0)
    hour_col = lax.broadcasted_iota(jnp.int32, (H_DEV, cols), 1)
    hour_of = ((hour_col >= hour_row * block) & (hour_col < hour_row * block + block)).astype(f32)
    small[...] = jnp.zeros_like(small)
    small[:, :units] = cons_ref[...]
    target[...] = jnp.dot(small[...].T, hour_of, preferred_element_type=f32, precision=lax.Precision.HIGHEST)
    small[...] = jnp.zeros_like(small)
    small[:table_ref.shape[0], :units] = table_ref[...]
    ut_ref[...] = small[...].T
    fac[pl.ds(pl.multiple_of(scen * rows, 16), rows), :] = sel_ref[...]
    tabs[scen] = tab_ref[...]
    ext[:up, :] = pw[...].astype(bf16)
    ext[up:, :] = wind_ref[...]
    needed = jnp.zeros((1, cols), f32)
    for h in range(H_DEV):
        needed = jnp.where(hour_of[h:h + 1] > 0.0, need_ref[h], needed)
    total_row[...] = jnp.sum(wind_ref[...].astype(f32), axis=0, keepdims=True) - needed
    send_edges(0)
    backs[...] = jnp.zeros((up, cols), f32)

    def along_z(k):
        for down in (True, False):
            zz = z - k if down else z + k
            ok = zz >= 0 if down else zz < n_z

            @pl.when(ok)
            def _():
                p = piece(zz, x, mine)
                arrived(p)
                if down:
                    @pl.when(z < n_z - 1)
                    def _():
                        pass_on(p, 1, dev_up)
                else:
                    @pl.when(z > 0)
                    def _():
                        pass_on(p, 0, dev_dn)
                pass_on(p, 2, dev_x)
                pass_on(p, 3, dev_y)
                pass_on(p, 4, dev_c)

    def both(k, f):
        @pl.when(z - k >= 0)
        def _():
            f(z - k)

        @pl.when(z + k < n_z)
        def _():
            f(z + k)

    def across_x(zz):
        p = piece(zz, ox, mine)
        arrived(p)
        pass_on(p, 3, dev_y)
        pass_on(p, 4, dev_c)

    def from_y_same(zz):
        p = piece(zz, x, other)
        arrived(p)
        pass_on(p, 4, dev_c)

    def from_y_cross(zz):
        p = piece(zz, ox, other)
        arrived(p)
        pass_on(p, 4, dev_c)

    def own_plane_x():
        for q in (mine, other):
            p = piece(z, ox, q)
            arrived(p)
            pass_on(p, 4, dev_c)

    def table_arrived(src):
        pltpu.make_async_remote_copy(
            src_ref=tab_ref, dst_ref=tabs.at[src], send_sem=tsend.at[0], recv_sem=trecv.at[src],
            device_id=dev_x, device_id_type=MESH).wait_recv()

    spread_row = lax.broadcasted_iota(jnp.int32, (H_DEV, cols), 0)
    spread_col = lax.broadcasted_iota(jnp.int32, (H_DEV, cols), 1)
    load_of = ((spread_col >= spread_row * block) & (spread_col < spread_row * block + block)).astype(bf16)
    lines_first = (((0,), (0,)), ((), ()))

    def line_step(at_rows):
        flows = jnp.dot(fac[at_rows, :], ext[...], preferred_element_type=f32) - load[at_rows, :]
        lim = bound[at_rows, :]
        exc[at_rows, :] = (flows - jnp.clip(flows, -lim, lim)).astype(bf16)

    def process(zz):
        for xx in range(2):
            s = zz * 2 + xx
            at_rows = pl.ds(pl.multiple_of(s * rows, 16), rows)
            load[at_rows, :] = lax.dot_general(tabs[s], load_of, lines_first, preferred_element_type=f32)
            bound[at_rows, :] = jnp.broadcast_to(fac[at_rows, units:units + 1].astype(f32), (rows, cols))
        at_rows = pl.ds(pl.multiple_of(zz * chunk, 128), chunk)
        fact[:, at_rows] = fac[at_rows, :up].T
        line_step(at_rows)
        backs[...] += jnp.dot(fact[:, at_rows], exc[at_rows, :], preferred_element_type=f32)

    def from_core(zz):
        for xx in range(2):
            for yy in range(2):
                arrived(piece(zz, xx, yy * 2 + oc))
            table_arrived(zz * 2 + xx)
        process(zz)

    def own_chunk():
        for q in (oc, 2 + oc):
            arrived(piece(z, ox, q))
        table_arrived(z * 2 + ox)
        process(z)

    along_z(1)
    own_plane_x()
    for k in range(2, n_z + 1):
        if k < n_z:
            along_z(k)
        both(k - 1, across_x)
        both(k - 1, from_y_same)
        if k > 2:
            both(k - 2, from_y_cross)
            both(k - 2, from_core)
        else:
            own_chunk()
    both(n_z - 1, from_y_cross)
    both(n_z - 1, from_core)

    tile = 32
    lane = lax.broadcasted_iota(jnp.int32, (tile, cols), 1)
    for number in range(PASSES):
        if number > 0:
            send_edges(number)
            for k in range(n_z):
                line_step(pl.ds(k * chunk, chunk))
            backs[...] = jnp.dot(fact[...], exc[...], preferred_element_type=f32)

        @pl.when(tm > 0)
        def _():
            edge_copy(number, 0).wait_recv()
            for g in range(4):
                e = erecv[number, 0]
                s = (-32 * g) % 128
                bef[g * (up // 4):(g + 1) * (up // 4), :] = pltpu.roll(e, s, 1) if s else e

        @pl.when(tm == 0)
        def _():
            bef[...] = pw[:, :128]

        @pl.when(tm < n_tm - 1)
        def _():
            edge_copy(number, 1).wait_recv()
            for g in range(4):
                e = erecv[number, 1]
                s = (96 - 32 * g) % 128
                aft[g * (up // 4):(g + 1) * (up // 4), :] = pltpu.roll(e, s, 1) if s else e

        @pl.when(tm == n_tm - 1)
        def _():
            aft[...] = pw[:, cols - 128:]

        balance = jnp.sum(pw[...], axis=0, keepdims=True) + total_row[...]
        balance_part = balance_weight * balance

        def update(i, carry):
            r = pl.ds(pl.multiple_of(i * tile, tile), tile)
            power = pw[r, :]
            commit = cm[r, :]
            linear = ut_ref[r, 0:1]
            quadratic = ut_ref[r, 1:2]
            capacity = ut_ref[r, 2:3]
            ramp_limit = ut_ref[r, 3:4]
            noload = ut_ref[r, 4:5]
            b = bef[r, :]
            a = aft[r, :]
            previous = jnp.where(lane < block, jnp.concatenate([b] * (cols // 128), axis=1), pltpu.roll(power, block, 1))
            nxt = jnp.where(lane >= cols - block, jnp.concatenate([a] * (cols // 128), axis=1), pltpu.roll(power, cols - block, 1))
            rate = power - previous
            over = rate - jnp.clip(rate, -ramp_limit, ramp_limit)
            coming = nxt - power
            following = coming - jnp.clip(coming, -ramp_limit, ramp_limit)
            ramp_term = over - following
            short = jnp.maximum(power - capacity * commit, 0.0)
            grad_power = (linear + 2.0 * quadratic * power + flow_weight * backs[r, :] + ramp_weight * ramp_term
                          + balance_part + short_weight * short)
            grad_commit = noload - short_weight * capacity * short + mult[r, :] + penalty * (commit - target[r, :])
            new_power = jnp.clip(power - step_power * grad_power, 0.0, capacity)
            pw[r, :] = new_power
            cm[r, :] = jnp.clip(commit - step_commit * grad_commit, 0.0, 1.0)
            ext[r, :] = new_power.astype(bf16)
            return carry

        lax.fori_loop(0, up // tile, update, 0, unroll=4)
        if number < PASSES - 1:
            store_edges(number + 1)

    spread = hour_of.astype(bf16)
    sums = jnp.zeros((H_DEV, up), f32)
    for part in split(cm[...] + mult[...] / penalty):
        sums = sums + lax.dot_general(spread, part, (((1,), (1,)), ((), ())), preferred_element_type=f32)
    psend[...] = sums

    def sum_copy(k):
        return pltpu.make_async_remote_copy(
            src_ref=psend, dst_ref=precv.at[scen], send_sem=psem_s.at[k], recv_sem=psem_r.at[scen],
            device_id=(tm, lax.rem(scen + k, n_scen)), device_id_type=MESH)

    for k in range(1, n_scen):
        sum_copy(k).start()
    precv[scen] = psend[...]
    power_out[...] = pw[:units, :]
    commit_out[...] = cm[:units, :]
    for k in range(1, n_scen):
        src = lax.rem(scen + k, n_scen)
        pltpu.make_async_remote_copy(
            src_ref=psend, dst_ref=precv.at[src], send_sem=psem_s.at[k], recv_sem=psem_r.at[src],
            device_id=dev_x, device_id_type=MESH).wait_recv()
    totals = precv[0]
    for k in range(1, n_scen):
        totals = totals + precv[k]
    consensus = jnp.clip(totals / (block * n_scen), 0.0, 1.0)
    cons_out[...] = consensus

    @pl.when(z > 0)
    def _():
        copy(own(mine), p_own, 0, dev_dn).wait_send()

    @pl.when(z < n_z - 1)
    def _():
        copy(own(mine), p_own, 1, dev_up).wait_send()

    copy(own(mine), p_own, 2, dev_x).wait_send()
    copy(own(other), p_own2, 2, dev_x).wait_send()

    def left(p, slot, dev):
        copy(at(p), p, slot, dev).wait_send()

    for k in range(1, n_z):
        for down in (True, False):
            zz = z - k if down else z + k

            @pl.when(zz >= 0 if down else zz < n_z)
            def _():
                p = piece(zz, x, mine)
                if down:
                    @pl.when(z < n_z - 1)
                    def _():
                        left(p, 1, dev_up)
                else:
                    @pl.when(z > 0)
                    def _():
                        left(p, 0, dev_dn)
                left(p, 2, dev_x)
                left(p, 3, dev_y)
                left(p, 4, dev_c)
                p = piece(zz, ox, mine)
                left(p, 3, dev_y)
                left(p, 4, dev_c)
                left(piece(zz, x, other), 4, dev_c)
                left(piece(zz, ox, other), 4, dev_c)
    for q in (mine, other):
        left(piece(z, ox, q), 4, dev_c)
    for k in range(1, n_scen):
        table_copy(k).wait_send()
        sum_copy(k).wait_send()
    for number in range(PASSES):
        @pl.when(tm < n_tm - 1)
        def _():
            edge_copy(number, 0).wait_send()

        @pl.when(tm > 0)
        def _():
            edge_copy(number, 1).wait_send()


def selection(unit_buses, wind_buses, buses, up, dtype):
    units = unit_buses.shape[0]
    wanted = jnp.concatenate([unit_buses, jnp.full((up - units,), -1, unit_buses.dtype), wind_buses])
    return (lax.broadcasted_iota(jnp.int32, (buses, wanted.shape[0]), 0) == wanted[None, :]).astype(dtype)


def finish(units, power_ref, commit_ref, mult_ref, cons_ref, power_out, commit_out, cons_out, upd_out, parts):
    tile, cols = mult_ref.shape
    block = cols // H_DEV
    step = pl.program_id(0)

    @pl.when(step == 0)
    def _():
        cons = cons_ref[...]
        cons_out[...] = cons[:, :units]
        parts[...] = jnp.concatenate([part.astype(jnp.float32) for part in split(cons)], axis=0).T

    hour_row = lax.broadcasted_iota(jnp.int32, (H_DEV, cols), 0)
    hour_col = lax.broadcasted_iota(jnp.int32, (H_DEV, cols), 1)
    hour_of = ((hour_col >= hour_row * block) & (hour_col < hour_row * block + block)).astype(jnp.float32)
    spread = jnp.concatenate([hour_of] * 3, axis=0).astype(jnp.bfloat16)
    mine = parts[pl.ds(pl.multiple_of(step * tile, 8), tile), :].astype(jnp.bfloat16)
    wide = jnp.dot(mine, spread, preferred_element_type=jnp.float32)
    power_out[...] = power_ref[...]
    commit = commit_ref[...]
    commit_out[...] = commit
    upd_out[...] = mult_ref[...] + penalty * (commit - wide)


def fused(n_tm, n_scen, prior_dispatch, prior_commitment, prior_consensus, prior_multiplier, flow_factors,
          unit_buses, wind_buses, wind_output, demand, load_flows, line_limits, unit_table):
    units, cols = prior_dispatch.shape
    rows, buses = flow_factors.shape
    farms = wind_output.shape[0]
    up = -(-units // 128) * 128
    f32, bf16 = jnp.float32, jnp.bfloat16
    sel = jnp.dot(flow_factors, selection(unit_buses, wind_buses, buses, up, bf16), preferred_element_type=f32).astype(bf16)
    column = lax.broadcasted_iota(jnp.int32, sel.shape, 1)
    sel = jnp.where(column == units, line_limits[:, None], sel)
    lines = rows * n_scen
    wide = up + farms
    vm = pl.BlockSpec(memory_space=pltpu.VMEM)
    dma = pltpu.SemaphoreType.DMA
    power, commit, cons = pl.pallas_call(
        functools.partial(kernel, n_tm, n_scen, units),
        name="window",
        out_shape=(
            jax.ShapeDtypeStruct((units, cols), f32),
            jax.ShapeDtypeStruct((units, cols), f32),
            jax.ShapeDtypeStruct((H_DEV, up), f32),
        ),
        in_specs=[vm] * 8 + [pl.BlockSpec(memory_space=pltpu.SMEM)],
        out_specs=(vm,) * 3,
        scratch_shapes=[
            pltpu.VMEM((lines, wide), bf16),
            pltpu.VMEM((up, lines), bf16),
            pltpu.VMEM((lines, cols), f32),
            pltpu.VMEM((lines, cols), f32),
            pltpu.VMEM((lines, cols), bf16),
            pltpu.VMEM((up, cols), f32),
            pltpu.VMEM((up, cols), f32),
            pltpu.VMEM((up, cols), f32),
            pltpu.VMEM((up, cols), f32),
            pltpu.VMEM((wide, cols), bf16),
            pltpu.VMEM((up, cols), f32),
            pltpu.VMEM((up, 128), f32),
            pltpu.VMEM((up, 128), f32),
            pltpu.VMEM((n_scen, H_DEV, rows), bf16),
            pltpu.VMEM((PASSES, 2, up // 4, 128), f32),
            pltpu.VMEM((PASSES, 2, up // 4, 128), f32),
            pltpu.VMEM((H_DEV, up), f32),
            pltpu.VMEM((n_scen, H_DEV, up), f32),
            pltpu.VMEM((1, cols), f32),
            pltpu.VMEM((H_DEV, up), f32),
            pltpu.VMEM((up, H_DEV), f32),
            dma((n_scen * 4,)),
            dma((5, n_scen * 4)),
            dma((n_scen,)),
            dma((n_scen,)),
            dma((PASSES, 2)),
            dma((PASSES, 2)),
            dma((n_scen,)),
            dma((n_scen,)),
        ],
        compiler_params=pltpu.CompilerParams(collective_id=0, has_side_effects=True, vmem_limit_bytes=56 * 1024 * 1024),
    )(sel, load_flows.T, prior_dispatch, prior_commitment, prior_consensus.T, prior_multiplier, wind_output, unit_table, demand)
    steps = 1
    tiles = pl.BlockSpec((units // steps, cols), lambda i: (i, 0))
    power, commit, cons, updated = pl.pallas_call(
        functools.partial(finish, units),
        name="finish",
        out_shape=(
            jax.ShapeDtypeStruct((units, cols), f32),
            jax.ShapeDtypeStruct((units, cols), f32),
            jax.ShapeDtypeStruct((H_DEV, units), f32),
            jax.ShapeDtypeStruct((units, cols), f32),
        ),
        grid=(steps,),
        in_specs=[tiles, tiles, tiles, pl.BlockSpec((H_DEV, up), lambda i: (0, 0))],
        out_specs=(tiles, tiles, pl.BlockSpec((H_DEV, units), lambda i: (0, 0)), tiles),
        scratch_shapes=[pltpu.VMEM((up, 3 * H_DEV), f32)],
    )(power, commit, prior_multiplier, cons)
    return power, commit, cons.T, updated


def passed_along(value, axis, steps):
    count = lax.axis_size(axis)
    first, last = (max(0, -steps), min(count, count - steps))
    return lax.ppermute(value, axis, [(source, source + steps) for source in range(first, last)])


def plain(prior_dispatch, prior_commitment, prior_consensus, prior_multiplier, flow_factors,
          unit_buses, wind_buses, wind_output, demand, load_flows, line_limits, unit_table):
    units, columns = prior_dispatch.shape
    block = columns // H_DEV
    linear, quadratic, capacity, ramp_limit, noload = (unit_table[i][:, None] for i in range(5))
    factors = jnp.dot(flow_factors, selection(unit_buses, wind_buses, flow_factors.shape[1], units, jnp.bfloat16),
                      preferred_element_type=jnp.float32).astype(jnp.bfloat16)
    wind_total = jnp.sum(wind_output.astype(jnp.float32), axis=0)
    needed = jnp.repeat(demand, block)
    target = jnp.repeat(prior_consensus, block, axis=1)
    first_block = lax.axis_index("tm") == 0
    last_block = lax.axis_index("tm") == lax.axis_size("tm") - 1
    power, commit = prior_dispatch, prior_commitment
    factors = lax.all_gather(factors, "scen", axis=0, tiled=True)
    hourly = jnp.repeat(lax.all_gather(load_flows, "scen", axis=0, tiled=True).astype(jnp.float32), block, axis=1)
    limit = lax.all_gather(line_limits, "scen", axis=0, tiled=True).astype(jnp.float32)[:, None]
    for _ in range(PASSES):
        extended = jnp.concatenate([power.astype(jnp.bfloat16), wind_output], axis=0)
        flows = jnp.dot(factors, extended, preferred_element_type=jnp.float32) - hourly
        excess = (flows - jnp.clip(flows, -limit, limit)).astype(jnp.bfloat16)
        back = lax.dot_general(factors[:, :units], excess, (((0,), (0,)), ((), ())), preferred_element_type=jnp.float32)
        before = passed_along(power[:, columns - block:], "tm", 1)
        after = passed_along(power[:, :block], "tm", -1)
        before = jnp.where(first_block, power[:, :block], before)
        after = jnp.where(last_block, power[:, columns - block:], after)
        rate = power - jnp.concatenate([before, power[:, :columns - block]], axis=1)
        coming = jnp.concatenate([power[:, block:], after], axis=1) - power
        over = rate - jnp.clip(rate, -ramp_limit, ramp_limit)
        following = coming - jnp.clip(coming, -ramp_limit, ramp_limit)
        balance = jnp.sum(power, axis=0) + wind_total - needed
        short = jnp.maximum(power - capacity * commit, 0.0)
        grad_power = (linear + 2.0 * quadratic * power + flow_weight * back + ramp_weight * (over - following)
                      + balance_weight * balance + short_weight * short)
        grad_commit = noload - short_weight * capacity * short + prior_multiplier + penalty * (commit - target)
        power, commit = (jnp.clip(power - step_power * grad_power, 0.0, capacity),
                         jnp.clip(commit - step_commit * grad_commit, 0.0, 1.0))
    sums = jnp.sum((commit + prior_multiplier / penalty).reshape(units, H_DEV, block), axis=2)
    totals = lax.psum(sums, "scen")
    consensus = jnp.clip(totals / (block * lax.axis_size("scen")), 0.0, 1.0)
    updated = prior_multiplier + penalty * (commit - jnp.repeat(consensus, block, axis=1))
    return power, commit, consensus, updated


def solution(mesh):
    n_tm, n_scen = mesh.shape["tm"], mesh.shape["scen"]

    def per_device(*args):
        rows, cols = args[4].shape[0], args[0].shape[1]
        fits = (n_tm == 4 and n_scen % 2 == 0 and rows % 64 == 0 and cols == 256
                and args[7].shape[0] % 128 == 0 and args[0].shape[0] % 128 > 0)
        if fits:
            return fused(n_tm, n_scen, *args)
        return plain(*args)

    both_axes = P(None, ("tm", "scen"))
    in_specs = (both_axes, both_axes, P(None, "tm"), both_axes, P("scen", None), P(), P(), both_axes,
                P("tm"), P("scen", "tm"), P("scen"), P())
    out_specs = (both_axes, both_axes, P(None, "tm"), both_axes)
    return jax.shard_map(per_device, mesh=mesh, in_specs=in_specs, out_specs=out_specs, check_vma=False)
```

profile of v0, /device:TPU:1, one launch (start us, length us, event | category | flops | bytes accessed | tf_op | source)
XLA Modules:
  0.0 62.1 jit_solution(2536757919389300870)
XLA Ops:
  0.6 0.0 copy-start
  0.7 0.9 %pad_add_fusion = s32[768]{0:T(1024)S(1)} fusion(s32[128]{0:T(128)} %param.18, s32[40]{0:T(128)S(1)} %broadcast_in_dim.14, s32[600]{0:T(1024)} %param.17), kind=kLoop, calls=%fused_computation.6 | loop fusion | flops 1536 | bytes 6144 | tf_op jit(solution)/shard_map/concatenate | solution.py:427
  1.5 0.4 copy-done
  2.0 2.9 %fusion.4.sel_ref = bf16[320,768]{1,0:T(8,128)(2,1)} fusion(bf16[320,2000]{1,0:T(8,128)(2,1)S(1)} %copy-done, s32[768]{0:T(1024)S(1)} %pad_add_fusion, pred[768]{0:T(1024)(128)(4,1)S(1)} %iota_compare_fusion.8, bf16[320]{0:T(512)(128)(2,1)} %param.22), kind=kOutput, calls=%fused_computation.5 | convolution fusion | flops 985067520 | bytes 1776000 | tf_op jit(solution)/shard_map/dot_general | solution.py:461
  4.8 54.4 %window.1 = (f32[600,256]{1,0:T(8,128)}, f32[600,256]{1,0:T(8,128)}, f32[8,640]{1,0:T(8,128)}) custom-call(bf16[320,768]{1,0:T(8,128)(2,1)} %fusion.4.sel_ref, bf16[8,320]{1,0:T(8,128)(2,1)} %bitcast.7, f32[600,256]{1,0:T(8,128)} %pd_ref.1, f32[600,256]{1,0:T(8,128)} %pc_ref.1, f32[8,600]{1,0:T(8,128)} %bitcast.6, f32[600,256]{1,0:T(8,128)} %mult_ref.1, ...), custom_call_target="tpu_custom_call" | custom-call | tf_op jit(solution)/shard_map/window/pallas_call | solution.py:468
  59.2 2.9 %finish.1 = (f32[600,256]{1,0:T(8,128)}, f32[600,256]{1,0:T(8,128)}, f32[8,600]{1,0:T(8,128)}, f32[600,256]{1,0:T(8,128)}) custom-call(f32[600,256]{1,0:T(8,128)} %get-tuple-element.11.power_ref, f32[600,256]{1,0:T(8,128)} %get-tuple-element.12.commit_ref, f32[600,256]{1,0:T(8,128)} %mult_ref.1, f32[8,640]{1,0:T(8,128)} %get-tuple-element.13.cons_ref), custom_call_target="tpu_custom_call" | custom-call | tf_op jit(solution)/shard_map/finish/pallas_call | solution.py:513
  (2 shorter events, 0.0 us)
Async XLA Ops:
  0.6 1.4 %copy-start = (bf16[320,2000]{1,0:T(8,128)(2,1)S(1)}, bf16[320,2000]{1,0:T(8,128)(2,1)}, u32[]{:S(2)}) copy-start(bf16[320,2000]{1,0:T(8,128)(2,1)} %param.16) | copy-start | bytes 3840004
where the time goes:
time: 62.4 us; the launch traced here: 62.1 us
  Pallas kernels  57.3 us (92%)
  matrix products  2.85 us (5%)
  other arithmetic  0.89 us (1%)
  between operations  0.66 us (1%)
    pallas_call x1, Pallas kernels, fused(): pl.pallas_call(functools.partial(kernel, n_tm, n_scen, units), name='wind...  54.4 us
    pallas_call x1, Pallas kernels, fused(): pl.pallas_call(functools.partial(finish, units), name='finish', out_shape...  2.91 us
    dot_general x1, matrix products, fused(): jnp.dot(flow_factors, selection(unit_buses, wind_buses, buses, up, bf16),...  2.85 us

commit v1 on v0

v1 whole, which is shorter than its diff:
```python
import functools

import jax
import jax.numpy as jnp
from jax import lax
from jax.experimental import pallas as pl
from jax.experimental.pallas import tpu as pltpu
from jax.sharding import PartitionSpec as P

PASSES = 3
H_DEV = 8
MESH = pl.DeviceIdType.MESH

flow_weight = 0.5
ramp_weight = 1.0
balance_weight = 0.004
short_weight = 2.0
penalty = 1.0
step_power = 0.2
step_commit = 0.3


def split(value):
    high = value.astype(jnp.bfloat16)
    rest = value - high.astype(jnp.float32)
    middle = rest.astype(jnp.bfloat16)
    return high, middle, (rest - middle.astype(jnp.float32)).astype(jnp.bfloat16)


def beyond(value, limit):
    return value - jnp.minimum(jnp.maximum(value, -limit), limit)


def kernel(n_tm, n_scen, units, fl_hbm, pd_hbm, pc_hbm, mu_hbm, wind_hbm, ub_ref, wb_ref, tab_ref, lim_ref, cons_ref,
           table_ref, need_ref,
           power_out, commit_out, mult_out, cons_out,
           fbuf, hot, ids, fac, fact, load, bound, exc, pw, cm, mult, off, part, ext, backs, bef, aft,
           keep, lin, cap, ramp, tabs, esend, erecv, psend, precv, wind_row, small,
           in_sem, out_sem, recv_sem, zsend, xsend, ysend, csend, tsend, trecv, esem_s, esem_r, psem_s, psem_r):
    rows, buses = fbuf.shape
    quarter = rows // 4
    up, cols = pw.shape
    half = cols // 2
    block = cols // H_DEV
    chunk = 2 * rows
    n_z = n_scen // 2
    f32, bf16 = jnp.float32, jnp.bfloat16
    tm = lax.axis_index("tm")
    scen = lax.axis_index("scen")
    y, c = tm // 2, tm % 2
    z, x = scen // 2, scen % 2
    oy = 1 - y
    oc = 1 - c
    ox = 1 - x
    mine = y * 2 + c
    other = oy * 2 + c
    dev_x = (tm, z * 2 + ox)
    dev_y = (oy * 2 + c, scen)
    dev_c = (y * 2 + oc, scen)

    load_in = [pltpu.make_async_copy(src, dst, in_sem.at[i]) for i, (src, dst) in enumerate((
        (fl_hbm, fbuf), (pd_hbm, pw.at[pl.ds(0, units), :]), (pc_hbm, cm.at[pl.ds(0, units), :]),
        (mu_hbm, mult.at[pl.ds(0, units), :]), (wind_hbm, ext.at[pl.ds(up, wind_hbm.shape[0]), :])))]
    for item in load_in:
        item.start()

    barrier = pltpu.get_barrier_semaphore()
    for k in range(1, n_scen):
        pl.semaphore_signal(barrier, inc=1, device_id=(tm, lax.rem(scen + k, n_scen)), device_id_type=MESH)
    for k in range(1, n_tm):
        pl.semaphore_signal(barrier, inc=1, device_id=(lax.rem(tm + k, n_tm), scen), device_id_type=MESH)

    first_rows = -(-quarter // 32) * 16
    starts = (0, first_rows)
    sizes = (first_rows, quarter - first_rows)

    def piece(zz, xx, q):
        return (zz * 2 + xx) * 4 + q

    def copy(p, h, sem, dev):
        ref = fac.at[pl.ds(pl.multiple_of(p * quarter + starts[h], 16), sizes[h]), :]
        return pltpu.make_async_remote_copy(
            src_ref=ref, dst_ref=ref, send_sem=sem, recv_sem=recv_sem.at[h, p],
            device_id=dev, device_id_type=MESH)

    def to_z(p, h, way):
        return copy(p, h, zsend.at[way, h, p], (tm, scen + 2 * (2 * way - 1)))

    def to_x(p, h):
        return copy(p, h, xsend.at[h, p], dev_x)

    def to_y(p, h):
        return copy(p, h, ysend.at[h, p], dev_y)

    def to_c(p, h):
        return copy(p, h, csend.at[h, p], dev_c)

    def arrived(p, h):
        to_x(p, h).wait_recv()

    def table_copy(k):
        peer = lax.rem(scen + k, n_scen)
        return pltpu.make_async_remote_copy(
            src_ref=tabs.at[scen], dst_ref=tabs.at[scen], send_sem=tsend.at[k], recv_sem=trecv.at[scen],
            device_id=(tm, peer), device_id_type=MESH)

    ids[...] = jnp.full(ids.shape, -1, jnp.int32)
    ids[0:1, :units] = ub_ref[...].reshape(1, units)
    ids[0:1, up:] = wb_ref[...].reshape(1, ids.shape[1] - up)
    step = 256
    number = lax.broadcasted_iota(jnp.int32, (step, ids.shape[1]), 0).astype(f32).astype(bf16)
    wanted = ids[0:1, :]
    one = jnp.ones((), bf16)
    for k in range(0, buses, step):
        here = jnp.where((wanted >= k) & (wanted < k + step), wanted - k, -1).astype(f32).astype(bf16)
        n = min(step, buses - k)
        hot[k:k + n, :] = jnp.where(number[:n] == here, one, one - one)
    tabs[scen] = jnp.concatenate(
        [tab_ref[...].astype(f32), jnp.broadcast_to(lim_ref[...].astype(f32).reshape(1, rows), (8, rows))], axis=0).astype(bf16)
    load_in[0].wait()

    def select(part_of):
        src = pl.ds(pl.multiple_of(part_of * 2 * quarter, 16), 2 * quarter)
        dst = pl.ds(pl.multiple_of(scen * rows + part_of * 2 * quarter, 16), 2 * quarter)
        fac[dst, :] = jnp.dot(fbuf[src, :], hot[...], preferred_element_type=f32).astype(bf16)

    select(y)
    pl.semaphore_wait(barrier, n_scen - 1 + n_tm - 1)

    p_own = piece(z, x, mine)

    def own_sends(f):
        for h in range(2):
            f(to_x(p_own, h))

            @pl.when(z > 0)
            def _():
                f(to_z(p_own, h, 0))

            @pl.when(z < n_z - 1)
            def _():
                f(to_z(p_own, h, 1))

    own_sends(lambda item: item.start())
    for k in range(1, n_scen):
        table_copy(k).start()

    def edges_of(tile_last, tile_first):
        lane = lax.broadcasted_iota(jnp.int32, (up // 4, 128), 1)
        last = jnp.zeros((up // 4, 128), f32)
        first = jnp.zeros((up // 4, 128), f32)
        for g in range(4):
            inside = (lane >= 32 * g) & (lane < 32 * g + 32)
            a = tile_last[g * (up // 4):(g + 1) * (up // 4), :]
            b = tile_first[g * (up // 4):(g + 1) * (up // 4), :]
            sa = (32 * g - 96) % 128
            sb = (32 * g) % 128
            a = pltpu.roll(a, sa, 1) if sa else a
            b = pltpu.roll(b, sb, 1) if sb else b
            last = jnp.where(inside, a, last)
            first = jnp.where(inside, b, first)
        return last, first

    def edge_copy(number, way):
        dev = (tm + 1, scen) if way == 0 else (tm - 1, scen)
        return pltpu.make_async_remote_copy(
            src_ref=esend.at[number, way], dst_ref=erecv.at[number, way],
            send_sem=esem_s.at[number, way], recv_sem=esem_r.at[number, way],
            device_id=dev, device_id_type=MESH)

    def send_edges(number):
        last, first = edges_of(pw[:, cols - 128:], pw[:, :128])
        esend[number, 0] = last
        esend[number, 1] = first

        @pl.when(tm < n_tm - 1)
        def _():
            edge_copy(number, 0).start()

        @pl.when(tm > 0)
        def _():
            edge_copy(number, 1).start()

    def take_edges(number):
        @pl.when(tm > 0)
        def _():
            edge_copy(number, 0).wait_recv()
            e = erecv[number, 0]
            for g in range(4):
                s = (-32 * g) % 128
                bef[g * (up // 4):(g + 1) * (up // 4), :] = pltpu.roll(e, s, 1) if s else e

        @pl.when(tm == 0)
        def _():
            bef[...] = pw[:, :128]

        @pl.when(tm < n_tm - 1)
        def _():
            edge_copy(number, 1).wait_recv()
            e = erecv[number, 1]
            for g in range(4):
                s = (96 - 32 * g) % 128
                aft[g * (up // 4):(g + 1) * (up // 4), :] = pltpu.roll(e, s, 1) if s else e

        @pl.when(tm == n_tm - 1)
        def _():
            aft[...] = pw[:, cols - 128:]

    for item in load_in[1:]:
        item.wait()
    tail = jnp.zeros((up - units, cols), f32)
    pw[units:, :] = tail
    cm[units:, :] = tail
    mult[units:, :] = tail
    send_edges(0)
    select(oy)

    hour_row = lax.broadcasted_iota(jnp.int32, (2 * H_DEV, cols), 0)
    hour_col = lax.broadcasted_iota(jnp.int32, (2 * H_DEV, cols), 1)
    hour_of = ((hour_col >= hour_row * block) & (hour_col < hour_row * block + block)).astype(f32)
    load_of = hour_of.astype(bf16)
    bound_of = (hour_row == H_DEV).astype(f32).astype(bf16)
    lines_first = (((0,), (0,)), ((), ()))

    small[...] = jnp.zeros_like(small)
    small[:, :units] = cons_ref[...]
    target = jnp.dot(small[...].T, hour_of[:H_DEV], preferred_element_type=f32, precision=lax.Precision.HIGHEST)
    small[...] = jnp.zeros_like(small)
    small[:table_ref.shape[0], :units] = table_ref[...]
    table = small[...].T
    keep[...] = jnp.broadcast_to(1.0 - 2.0 * step_power * table[:, 1:2], keep.shape)
    lin[...] = jnp.broadcast_to(step_power * table[:, 0:1], lin.shape)
    cap[...] = jnp.broadcast_to(table[:, 2:3], cap.shape)
    ramp[...] = jnp.broadcast_to(table[:, 3:4], ramp.shape)
    off[...] = step_commit * (table[:, 4:5] + mult[...] - penalty * target)
    ext[:up, :] = pw[...].astype(bf16)
    needed = jnp.zeros((1, cols), f32)
    for h in range(H_DEV):
        needed = jnp.where(hour_of[h:h + 1] > 0.0, need_ref[h], needed)
    wind_row[...] = jnp.sum(ext[up:, :].astype(f32), axis=0, keepdims=True) - needed
    backs[...] = jnp.zeros((up, cols), f32)

    tile = 32
    lane = lax.broadcasted_iota(jnp.int32, (tile, half), 1)

    def start_next(r, p, both):
        capacity = cap[r, :]
        for i in range(2):
            h = pl.ds(i * half, half)
            commit = cm[r, h]
            short = jnp.maximum(p[i] - capacity * commit, 0.0)
            part[r, h] = p[i] * keep[r, :] - lin[r, :] - (step_power * short_weight) * short
            cm[r, h] = jnp.clip((1.0 - step_commit * penalty) * commit - off[r, h]
                                + (step_commit * short_weight) * capacity * short, 0.0, 1.0)

    def first_part(i, total):
        r = pl.ds(pl.multiple_of(i * tile, tile), tile)
        p = (pw[r, :half], pw[r, half:])
        start_next(r, p, True)
        both = jnp.concatenate(p, axis=1)
        return total + sum(both[8 * j:8 * j + 8] for j in range(tile // 8))

    def add_ramp(balance):
        for i in range(up // tile):
            r = pl.ds(i * tile, tile)
            p0, p1 = pw[r, :half], pw[r, half:]
            limit = ramp[r, :]
            r0, r1 = pltpu.roll(p0, block, 1), pltpu.roll(p1, block, 1)
            o0 = beyond(p0 - jnp.where(lane < block, bef[r, :], r0), limit)
            o1 = beyond(p1 - jnp.where(lane < block, r0, r1), limit)
            o2 = beyond(aft[r, :] - p1, limit)
            s0, s1 = pltpu.roll(o0, half - block, 1), pltpu.roll(o1, half - block, 1)
            f0 = jnp.where(lane >= half - block, s1, s0)
            f1 = jnp.where(lane >= half - block, o2, s1)
            part[r, :half] = part[r, :half] - (step_power * ramp_weight) * (o0 - f0) - balance[:, :half]
            part[r, half:] = part[r, half:] - (step_power * ramp_weight) * (o1 - f1) - balance[:, half:]

    def settle(last):
        def body(i, total):
            r = pl.ds(pl.multiple_of(i * tile, tile), tile)
            capacity = cap[r, :]
            p = []
            for j in range(2):
                h = pl.ds(j * half, half)
                p.append(jnp.minimum(jnp.maximum(part[r, h] - (step_power * flow_weight) * backs[r, h], 0.0), capacity))
                if last:
                    power_out_tile(r, h, p[j])
                else:
                    pw[r, h] = p[j]
                    ext[r, h] = p[j].astype(bf16)
            if last:
                return total
            start_next(r, p, True)
            both = jnp.concatenate(p, axis=1)
            return total + sum(both[8 * j:8 * j + 8] for j in range(tile // 8))
        return lax.fori_loop(0, up // tile, body, jnp.zeros((8, cols), f32), unroll=2)

    def power_out_tile(r, h, value):
        pw[r, h] = value

    def balance_of(total):
        return (step_power * balance_weight) * (jnp.sum(total, axis=0, keepdims=True) + wind_row[...])

    total = lax.fori_loop(0, up // tile, first_part, jnp.zeros((8, cols), f32), unroll=2)

    def line_step(at_rows):
        flows = jnp.dot(fac[at_rows, :], ext[...], preferred_element_type=f32) - load[at_rows, :]
        exc[at_rows, :] = beyond(flows, bound[at_rows, :]).astype(bf16)

    def process(zz):
        for xx in range(2):
            s = zz * 2 + xx
            at_rows = pl.ds(pl.multiple_of(s * rows, 16), rows)
            load[at_rows, :] = lax.dot_general(tabs[s], load_of, lines_first, preferred_element_type=f32)
            bound[at_rows, :] = lax.dot_general(tabs[s], bound_of, lines_first, preferred_element_type=f32)
        at_rows = pl.ds(pl.multiple_of(zz * chunk, 128), chunk)
        fact[:, at_rows] = fac[at_rows, :up].T
        line_step(at_rows)
        backs[...] += jnp.dot(fact[:, at_rows], exc[at_rows, :], preferred_element_type=f32)

    def table_arrived(src):
        pltpu.make_async_remote_copy(
            src_ref=tabs.at[src], dst_ref=tabs.at[src], send_sem=tsend.at[0], recv_sem=trecv.at[src],
            device_id=dev_x, device_id_type=MESH).wait_recv()

    def both(k, f, *rest):
        if k >= n_z:
            return

        @pl.when(z - k >= 0)
        def _():
            f(z - k, *rest)

        @pl.when(z + k < n_z)
        def _():
            f(z + k, *rest)

    def from_z(k, h):
        if k >= n_z:
            return
        for way in range(2):
            zz = z - k if way else z + k

            @pl.when(zz >= 0 if way else zz < n_z)
            def _():
                p = piece(zz, x, mine)
                arrived(p, h)

                @pl.when(z < n_z - 1 if way else z > 0)
                def _():
                    to_z(p, h, way).start()
                to_x(p, h).start()
                to_y(p, h).start()
                to_c(p, h).start()

    def from_xy(zz, h):
        p = piece(zz, ox, mine)
        arrived(p, h)

        @pl.when(c == 0)
        def _():
            to_y(p, h).start()
        to_c(p, h).start()
        p = piece(zz, x, other)
        arrived(p, h)

        @pl.when(c == 1)
        def _():
            to_x(p, h).start()
        to_c(p, h).start()

    def from_corner(zz, h):
        p = piece(zz, ox, other)
        arrived(p, h)
        to_c(p, h).start()

    def own_x(h):
        p = piece(z, ox, mine)
        arrived(p, h)
        to_y(p, h).start()
        to_c(p, h).start()

    def from_core(zz):
        for xx in range(2):
            for yy in range(2):
                for h in range(2):
                    arrived(piece(zz, xx, yy * 2 + oc), h)
            table_arrived(zz * 2 + xx)
        process(zz)

    def own_chunk():
        for q in (oc, 2 + oc):
            for h in range(2):
                arrived(piece(z, ox, q), h)
        table_arrived(z * 2 + ox)
        process(z)

    for h in range(2):
        own_x(h)
        from_z(1, h)
    take_edges(0)
    add_ramp(balance_of(total))
    for k in range(2, n_z + 2):
        for h in range(2):
            from_z(k, h)
            if k == 2:
                from_corner(z, h)
            both(k - 1, from_xy, h)
            if k > 2:
                both(k - 2, from_corner, h)
        if k == 3:
            own_chunk()
        if k > 3:
            both(k - 3, from_core)
    both(n_z - 1, from_core)

    total = settle(False)
    spread = hour_of[:H_DEV].astype(bf16)

    def sum_copy(k):
        return pltpu.make_async_remote_copy(
            src_ref=psend, dst_ref=precv.at[scen], send_sem=psem_s.at[k], recv_sem=psem_r.at[scen],
            device_id=(tm, lax.rem(scen + k, n_scen)), device_id_type=MESH)

    def put(i, src, dst):
        return pltpu.make_async_copy(src, dst, out_sem.at[i])

    put_commit = put(0, cm.at[pl.ds(0, units), :], commit_out)
    put_mult = put(1, mult.at[pl.ds(0, units), :], mult_out)
    put_power = put(2, pw.at[pl.ds(0, units), :], power_out)
    for number in range(1, PASSES):
        send_edges(number)
        final = number == PASSES - 1
        if final:
            put_commit.start()
            sums = jnp.zeros((H_DEV, up), f32)
            for item in split(cm[...] + mult[...] / penalty):
                sums = sums + lax.dot_general(spread, item, (((1,), (1,)), ((), ())), preferred_element_type=f32)
            psend[...] = sums
            for k in range(1, n_scen):
                sum_copy(k).start()
        for k in range(n_z):
            line_step(pl.ds(k * chunk, chunk))
        take_edges(number)
        add_ramp(balance_of(total))
        backs[...] = jnp.dot(fact[...], exc[...], preferred_element_type=f32)
        if final:
            precv[scen] = psend[...]
            for k in range(1, n_scen):
                src = lax.rem(scen + k, n_scen)
                pltpu.make_async_remote_copy(
                    src_ref=psend, dst_ref=precv.at[src], send_sem=psem_s.at[k], recv_sem=psem_r.at[src],
                    device_id=dev_x, device_id_type=MESH).wait_recv()
            totals = precv[0]
            for k in range(1, n_scen):
                totals = totals + precv[k]
            consensus = jnp.clip(totals / (block * n_scen), 0.0, 1.0)
            cons_out[...] = consensus[:, :units]
            pieces = jnp.concatenate([item.astype(f32) for item in split(consensus)], axis=0).T.astype(bf16)
            three = jnp.concatenate([hour_of[:H_DEV]] * 3, axis=0).astype(bf16)
            wide = jnp.dot(pieces, three, preferred_element_type=f32)
            mult[...] = mult[...] + penalty * (cm[...] - wide)
            put_mult.start()
        total = settle(final)
    put_power.start()

    own_sends(lambda item: item.wait_send())
    for h in range(2):
        p = piece(z, ox, mine)
        to_y(p, h).wait_send()
        to_c(p, h).wait_send()
        to_c(piece(z, ox, other), h).wait_send()

    def drain(k, way):
        zz = z - k if way else z + k

        @pl.when(zz >= 0 if way else zz < n_z)
        def _():
            for h in range(2):
                p = piece(zz, x, mine)

                @pl.when(z < n_z - 1 if way else z > 0)
                def _():
                    to_z(p, h, way).wait_send()
                to_x(p, h).wait_send()
                to_y(p, h).wait_send()
                to_c(p, h).wait_send()
                to_c(piece(zz, ox, mine), h).wait_send()
                to_c(piece(zz, x, other), h).wait_send()
                to_c(piece(zz, ox, other), h).wait_send()

                @pl.when(c == 0)
                def _():
                    to_y(piece(zz, ox, mine), h).wait_send()

                @pl.when(c == 1)
                def _():
                    to_x(piece(zz, x, other), h).wait_send()

    for k in range(1, n_z):
        for way in range(2):
            drain(k, way)
    for k in range(1, n_scen):
        table_copy(k).wait_send()
        sum_copy(k).wait_send()
    put_commit.wait()
    put_mult.wait()
    put_power.wait()
    for number in range(PASSES):
        @pl.when(tm < n_tm - 1)
        def _():
            edge_copy(number, 0).wait_send()

        @pl.when(tm > 0)
        def _():
            edge_copy(number, 1).wait_send()


def selection(unit_buses, wind_buses, buses, up, dtype):
    units = unit_buses.shape[0]
    wanted = jnp.concatenate([unit_buses, jnp.full((up - units,), -1, unit_buses.dtype), wind_buses])
    return (lax.broadcasted_iota(jnp.int32, (buses, wanted.shape[0]), 0) == wanted[None, :]).astype(dtype)


def finish(power_ref, commit_ref, mult_ref, cons_ref, power_out, commit_out, mult_out, cons_out):
    power_out[...] = power_ref[...]
    commit_out[...] = commit_ref[...]
    mult_out[...] = mult_ref[...]
    cons_out[...] = cons_ref[...]


def fused(n_tm, n_scen, prior_dispatch, prior_commitment, prior_consensus, prior_multiplier, flow_factors,
          unit_buses, wind_buses, wind_output, demand, load_flows, line_limits, unit_table):
    units, cols = prior_dispatch.shape
    rows, buses = flow_factors.shape
    farms = wind_output.shape[0]
    up = -(-units // 128) * 128
    f32, bf16 = jnp.float32, jnp.bfloat16
    lines = rows * n_scen
    wide = up + farms
    vm = pl.BlockSpec(memory_space=pltpu.VMEM)
    hbm = pl.BlockSpec(memory_space=pl.ANY)
    dma = pltpu.SemaphoreType.DMA
    shapes = (
        jax.ShapeDtypeStruct((units, cols), f32),
        jax.ShapeDtypeStruct((units, cols), f32),
        jax.ShapeDtypeStruct((units, cols), f32),
        jax.ShapeDtypeStruct((H_DEV, units), f32),
    )
    outs = pl.pallas_call(
        functools.partial(kernel, n_tm, n_scen, units),
        name="window",
        out_shape=shapes,
        in_specs=[hbm] * 5 + [vm] * 6 + [pl.BlockSpec(memory_space=pltpu.SMEM)],
        out_specs=(hbm, hbm, hbm, vm),
        scratch_shapes=[
            pltpu.VMEM((rows, buses), bf16),
            pltpu.VMEM((buses, wide), bf16),
            pltpu.VMEM((8, wide), jnp.int32),
            pltpu.VMEM((lines, wide), bf16),
            pltpu.VMEM((up, lines), bf16),
            pltpu.VMEM((lines, cols), f32),
            pltpu.VMEM((lines, cols), f32),
            pltpu.VMEM((lines, cols), bf16),
            pltpu.VMEM((up, cols), f32),
            pltpu.VMEM((up, cols), f32),
            pltpu.VMEM((up, cols), f32),
            pltpu.VMEM((up, cols), f32),
            pltpu.VMEM((up, cols), f32),
            pltpu.VMEM((wide, cols), bf16),
            pltpu.VMEM((up, cols), f32),
            pltpu.VMEM((up, 128), f32),
            pltpu.VMEM((up, 128), f32),
            pltpu.VMEM((up, 128), f32),
            pltpu.VMEM((up, 128), f32),
            pltpu.VMEM((up, 128), f32),
            pltpu.VMEM((up, 128), f32),
            pltpu.VMEM((n_scen, 2 * H_DEV, rows), bf16),
            pltpu.VMEM((PASSES, 2, up // 4, 128), f32),
            pltpu.VMEM((PASSES, 2, up // 4, 128), f32),
            pltpu.VMEM((H_DEV, up), f32),
            pltpu.VMEM((n_scen, H_DEV, up), f32),
            pltpu.VMEM((1, cols), f32),
            pltpu.VMEM((H_DEV, up), f32),
            dma((5,)),
            dma((3,)),
            dma((2, n_scen * 4)),
            dma((2, 2, n_scen * 4)),
            dma((2, n_scen * 4)),
            dma((2, n_scen * 4)),
            dma((2, n_scen * 4)),
            dma((n_scen,)),
            dma((n_scen,)),
            dma((PASSES, 2)),
            dma((PASSES, 2)),
            dma((n_scen,)),
            dma((n_scen,)),
        ],
        compiler_params=pltpu.CompilerParams(collective_id=0, has_side_effects=True, vmem_limit_bytes=56 * 1024 * 1024),
    )(flow_factors, prior_dispatch, prior_commitment, prior_multiplier, wind_output,
      unit_buses, wind_buses, load_flows.T, line_limits,
      prior_consensus.T, unit_table, demand)
    power, commit, updated, cons = pl.pallas_call(
        finish,
        name="finish",
        out_shape=shapes,
        in_specs=[vm] * 4,
        out_specs=(vm,) * 4,
    )(*outs)
    return power, commit, cons.T, updated


def passed_along(value, axis, steps):
    count = lax.axis_size(axis)
    first, last = (max(0, -steps), min(count, count - steps))
    return lax.ppermute(value, axis, [(source, source + steps) for source in range(first, last)])


def plain(prior_dispatch, prior_commitment, prior_consensus, prior_multiplier, flow_factors,
          unit_buses, wind_buses, wind_output, demand, load_flows, line_limits, unit_table):
    units, columns = prior_dispatch.shape
    block = columns // H_DEV
    linear, quadratic, capacity, ramp_limit, noload = (unit_table[i][:, None] for i in range(5))
    factors = jnp.dot(flow_factors, selection(unit_buses, wind_buses, flow_factors.shape[1], units, jnp.bfloat16),
                      preferred_element_type=jnp.float32).astype(jnp.bfloat16)
    wind_total = jnp.sum(wind_output.astype(jnp.float32), axis=0)
    needed = jnp.repeat(demand, block)
    target = jnp.repeat(prior_consensus, block, axis=1)
    first_block = lax.axis_index("tm") == 0
    last_block = lax.axis_index("tm") == lax.axis_size("tm") - 1
    power, commit = prior_dispatch, prior_commitment
    factors = lax.all_gather(factors, "scen", axis=0, tiled=True)
    hourly = jnp.repeat(lax.all_gather(load_flows, "scen", axis=0, tiled=True).astype(jnp.float32), block, axis=1)
    limit = lax.all_gather(line_limits, "scen", axis=0, tiled=True).astype(jnp.float32)[:, None]
    for _ in range(PASSES):
        extended = jnp.concatenate([power.astype(jnp.bfloat16), wind_output], axis=0)
        flows = jnp.dot(factors, extended, preferred_element_type=jnp.float32) - hourly
        excess = (flows - jnp.clip(flows, -limit, limit)).astype(jnp.bfloat16)
        back = lax.dot_general(factors[:, :units], excess, (((0,), (0,)), ((), ())), preferred_element_type=jnp.float32)
        before = passed_along(power[:, columns - block:], "tm", 1)
        after = passed_along(power[:, :block], "tm", -1)
        before = jnp.where(first_block, power[:, :block], before)
        after = jnp.where(last_block, power[:, columns - block:], after)
        rate = power - jnp.concatenate([before, power[:, :columns - block]], axis=1)
        coming = jnp.concatenate([power[:, block:], after], axis=1) - power
        over = rate - jnp.clip(rate, -ramp_limit, ramp_limit)
        following = coming - jnp.clip(coming, -ramp_limit, ramp_limit)
        balance = jnp.sum(power, axis=0) + wind_total - needed
        short = jnp.maximum(power - capacity * commit, 0.0)
        grad_power = (linear + 2.0 * quadratic * power + flow_weight * back + ramp_weight * (over - following)
                      + balance_weight * balance + short_weight * short)
        grad_commit = noload - short_weight * capacity * short + prior_multiplier + penalty * (commit - target)
        power, commit = (jnp.clip(power - step_power * grad_power, 0.0, capacity),
                         jnp.clip(commit - step_commit * grad_commit, 0.0, 1.0))
    sums = jnp.sum((commit + prior_multiplier / penalty).reshape(units, H_DEV, block), axis=2)
    totals = lax.psum(sums, "scen")
    consensus = jnp.clip(totals / (block * lax.axis_size("scen")), 0.0, 1.0)
    updated = prior_multiplier + penalty * (commit - jnp.repeat(consensus, block, axis=1))
    return power, commit, consensus, updated


def solution(mesh):
    n_tm, n_scen = mesh.shape["tm"], mesh.shape["scen"]

    def per_device(*args):
        rows, cols = args[4].shape[0], args[0].shape[1]
        fits = (n_tm == 4 and n_scen % 2 == 0 and rows % 64 == 0 and cols == 256
                and args[7].shape[0] % 128 == 0 and args[0].shape[0] % 128 > 0)
        if fits:
            return fused(n_tm, n_scen, *args)
        return plain(*args)

    both_axes = P(None, ("tm", "scen"))
    in_specs = (both_axes, both_axes, P(None, "tm"), both_axes, P("scen", None), P(), P(), both_axes,
                P("tm"), P("scen", "tm"), P("scen"), P())
    out_specs = (both_axes, both_axes, P(None, "tm"), both_axes)
    return jax.shard_map(per_device, mesh=mesh, in_specs=in_specs, out_specs=out_specs, check_vma=False)
```

time: 62.4 us -> 50.9 us (0.82)
  Pallas kernels: 57.3 us -> 50 us
  matrix products: 2.85 us -> 0 us
  other arithmetic: 0.89 us -> 0 us
    pallas_call x1, Pallas kernels: 54.4 us -> 47.3 us  [fused(): pl.pallas_call(functools.partial(kernel, n_tm, n_scen, units), name='wind...]
    dot_general x1 -> x0, matrix products: 2.85 us -> none  [fused(): jnp.dot(flow_factors, selection(unit_buses, wind_buses, buses, up, bf16),...]
    concatenate x1 -> x0, other arithmetic: 0.88 us -> none  [selection(): jnp.concatenate([unit_buses, jnp.full((up - units,), -1, unit_buses.dtype...]
where the time goes in v1:
time: 50.9 us; the launch traced here: 50.7 us
  Pallas kernels  50 us (98%)
  between operations  0.64 us (1%)
    pallas_call x1, Pallas kernels, fused(): pl.pallas_call(functools.partial(kernel, n_tm, n_scen, units), name='wind...  47.3 us
    pallas_call x1, Pallas kernels, fused(): pl.pallas_call(finish, name='finish', out_shape=shapes, in_specs=[vm] * 4...  2.72 us

profile of v1, /device:TPU:1, one launch (start us, length us, event | category | flops | bytes accessed | tf_op | source)
XLA Modules:
  0.0 50.7 jit_solution(8482266457095508364)
XLA Ops:
  0.6 47.3 %window.1 = (f32[600,256]{1,0:T(8,128)}, f32[600,256]{1,0:T(8,128)}, f32[600,256]{1,0:T(8,128)}, f32[8,600]{1,0:T(8,128)}) custom-call(bf16[320,2000]{1,0:T(8,128)(2,1)} %fl_hbm.1, f32[600,256]{1,0:T(8,128)} %pd_hbm.1, f32[600,256]{1,0:T(8,128)} %pc_hbm.1, f32[600,256]{1,0:T(8,128)} %mu_hbm.1, bf16[128,256]{1,0:T(8,128)(2,1)} %wind_hbm.1, s32[600]{0:T(1024)} %ub_ref.1, ...), custom_call_target="tpu_custom_call" | custom-call | tf_op jit(solution)/shard_map/window/pallas_call | solution.py:550
  47.9 2.7 %finish.1 = (f32[600,256]{1,0:T(8,128)}, f32[600,256]{1,0:T(8,128)}, f32[600,256]{1,0:T(8,128)}, f32[8,600]{1,0:T(8,128)}) custom-call(f32[600,256]{1,0:T(8,128)} %get-tuple-element.12.power_ref, f32[600,256]{1,0:T(8,128)} %get-tuple-element.13.commit_ref, f32[600,256]{1,0:T(8,128)} %get-tuple-element.14.mult_ref, f32[8,600]{1,0:T(8,128)} %get-tuple-element.15.cons_ref), custom_call_target="tpu_custom_call" | custom-call | tf_op jit(solution)/shard_map/finish/pallas_call | solution.py:603

commit v2 on v1

--- a/solution.py
+++ b/solution.py
@@ -36,7 +36,7 @@
            power_out, commit_out, mult_out, cons_out,
            fbuf, hot, ids, fac, fact, load, bound, exc, pw, cm, mult, off, part, ext, backs, bef, aft,
            keep, lin, cap, ramp, tabs, esend, erecv, psend, precv, wind_row, small,
-           in_sem, out_sem, recv_sem, zsend, xsend, ysend, csend, tsend, trecv, esem_s, esem_r, psem_s, psem_r):
+           in_sem, out_sem, recv_sem, crecv, zsend, xsend, ysend, csend, tsend, trecv, esem_s, esem_r, psem_s, psem_r):
     rows, buses = fbuf.shape
     quarter = rows // 4
     up, cols = pw.shape
@@ -71,32 +71,36 @@
         pl.semaphore_signal(barrier, inc=1, device_id=(lax.rem(tm + k, n_tm), scen), device_id_type=MESH)
 
     first_rows = -(-quarter // 32) * 16
-    starts = (0, first_rows)
-    sizes = (first_rows, quarter - first_rows)
+    starts = (0, first_rows, 0)
+    sizes = (first_rows, quarter - first_rows, quarter)
+    whole = 2
 
     def piece(zz, xx, q):
         return (zz * 2 + xx) * 4 + q
 
-    def copy(p, h, sem, dev):
+    def copy(p, h, sem, dev, got=None):
         ref = fac.at[pl.ds(pl.multiple_of(p * quarter + starts[h], 16), sizes[h]), :]
         return pltpu.make_async_remote_copy(
-            src_ref=ref, dst_ref=ref, send_sem=sem, recv_sem=recv_sem.at[h, p],
+            src_ref=ref, dst_ref=ref, send_sem=sem, recv_sem=recv_sem.at[h % 2, p // 8 * 4 + p // 4 % 2 * 2 + p % 4 // 2] if got is None else got,
             device_id=dev, device_id_type=MESH)
 
     def to_z(p, h, way):
-        return copy(p, h, zsend.at[way, h, p], (tm, scen + 2 * (2 * way - 1)))
+        return copy(p, h, zsend.at[way, p // 8], (tm, scen + 2 * (2 * way - 1)))
 
     def to_x(p, h):
-        return copy(p, h, xsend.at[h, p], dev_x)
+        return copy(p, h, xsend.at[p // 8 * 2 + (p % 4) // 2 * y + (1 - (p % 4) // 2) * (1 - y)], dev_x)
 
     def to_y(p, h):
-        return copy(p, h, ysend.at[h, p], dev_y)
+        return copy(p, h, ysend.at[p // 4], dev_y)
 
     def to_c(p, h):
-        return copy(p, h, csend.at[h, p], dev_c)
+        return copy(p, h, csend.at[p // 2], dev_c, crecv.at[p // 2])
 
     def arrived(p, h):
         to_x(p, h).wait_recv()
+
+    def from_partner(p):
+        to_c(p, whole).wait_recv()
 
     def table_copy(k):
         peer = lax.rem(scen + k, n_scen)
@@ -129,8 +133,8 @@
 
     p_own = piece(z, x, mine)
 
-    def own_sends(f):
-        for h in range(2):
+    def own_sends(f, parts):
+        for h in parts:
             f(to_x(p_own, h))
 
             @pl.when(z > 0)
@@ -141,7 +145,7 @@
             def _():
                 f(to_z(p_own, h, 1))
 
-    own_sends(lambda item: item.start())
+    own_sends(lambda item: item.start(), range(2))
     for k in range(1, n_scen):
         table_copy(k).start()
 
@@ -260,20 +264,28 @@
         both = jnp.concatenate(p, axis=1)
         return total + sum(both[8 * j:8 * j + 8] for j in range(tile // 8))
 
-    def add_ramp(balance):
-        for i in range(up // tile):
+    def add_ramp(balance, first=0, last=up // tile):
+        for i in range(first, last):
             r = pl.ds(i * tile, tile)
             p0, p1 = pw[r, :half], pw[r, half:]
             limit = ramp[r, :]
             r0, r1 = pltpu.roll(p0, block, 1), pltpu.roll(p1, block, 1)
-            o0 = beyond(p0 - jnp.where(lane < block, bef[r, :], r0), limit)
+            o0 = beyond(p0 - jnp.where(lane < block, p0, r0), limit)
             o1 = beyond(p1 - jnp.where(lane < block, r0, r1), limit)
-            o2 = beyond(aft[r, :] - p1, limit)
             s0, s1 = pltpu.roll(o0, half - block, 1), pltpu.roll(o1, half - block, 1)
             f0 = jnp.where(lane >= half - block, s1, s0)
-            f1 = jnp.where(lane >= half - block, o2, s1)
+            f1 = jnp.where(lane >= half - block, 0.0, s1)
             part[r, :half] = part[r, :half] - (step_power * ramp_weight) * (o0 - f0) - balance[:, :half]
             part[r, half:] = part[r, half:] - (step_power * ramp_weight) * (o1 - f1) - balance[:, half:]
+
+    def add_edges():
+        for i in range(up // tile):
+            r = pl.ds(i * tile, tile)
+            limit = ramp[r, :]
+            before = jnp.where(lane < block, beyond(pw[r, :half] - bef[r, :], limit), 0.0)
+            after = jnp.where(lane >= half - block, beyond(aft[r, :] - pw[r, half:], limit), 0.0)
+            part[r, :half] = part[r, :half] - (step_power * ramp_weight) * before
+            part[r, half:] = part[r, half:] + (step_power * ramp_weight) * after
 
     def settle(last):
         def body(i, total):
@@ -308,11 +320,6 @@
         exc[at_rows, :] = beyond(flows, bound[at_rows, :]).astype(bf16)
 
     def process(zz):
-        for xx in range(2):
-            s = zz * 2 + xx
-            at_rows = pl.ds(pl.multiple_of(s * rows, 16), rows)
-            load[at_rows, :] = lax.dot_general(tabs[s], load_of, lines_first, preferred_element_type=f32)
-            bound[at_rows, :] = lax.dot_general(tabs[s], bound_of, lines_first, preferred_element_type=f32)
         at_rows = pl.ds(pl.multiple_of(zz * chunk, 128), chunk)
         fact[:, at_rows] = fac[at_rows, :up].T
         line_step(at_rows)
@@ -383,16 +390,12 @@
     def from_core(zz):
         for xx in range(2):
             for yy in range(2):
-                for h in range(2):
-                    arrived(piece(zz, xx, yy * 2 + oc), h)
-            table_arrived(zz * 2 + xx)
+                from_partner(piece(zz, xx, yy * 2 + oc))
         process(zz)
 
     def own_chunk():
         for q in (oc, 2 + oc):
-            for h in range(2):
-                arrived(piece(z, ox, q), h)
-        table_arrived(z * 2 + ox)
+            from_partner(piece(z, ox, q))
         process(z)
 
     for h in range(2):
@@ -400,6 +403,13 @@
         from_z(1, h)
     take_edges(0)
     add_ramp(balance_of(total))
+    add_edges()
+    for k in range(1, n_scen):
+        table_arrived(lax.rem(scen + k, n_scen))
+    for s in range(n_scen):
+        at_rows = pl.ds(s * rows, rows)
+        load[at_rows, :] = lax.dot_general(tabs[s], load_of, lines_first, preferred_element_type=f32)
+        bound[at_rows, :] = lax.dot_general(tabs[s], bound_of, lines_first, preferred_element_type=f32)
     for k in range(2, n_z + 2):
         for h in range(2):
             from_z(k, h)
@@ -439,11 +449,16 @@
             psend[...] = sums
             for k in range(1, n_scen):
                 sum_copy(k).start()
+        balance = balance_of(total)
+        tiles = up // tile
         for k in range(n_z):
             line_step(pl.ds(k * chunk, chunk))
+            add_ramp(balance, tiles * k // n_z, tiles * (k + 1) // n_z)
         take_edges(number)
-        add_ramp(balance_of(total))
-        backs[...] = jnp.dot(fact[...], exc[...], preferred_element_type=f32)
+        add_edges()
+        for m in range(2):
+            r = pl.ds(m * (up // 2), up // 2)
+            backs[r, :] = jnp.dot(fact[r, :], exc[...], preferred_element_type=f32)
         if final:
             precv[scen] = psend[...]
             for k in range(1, n_scen):
@@ -464,8 +479,8 @@
         total = settle(final)
     put_power.start()
 
-    own_sends(lambda item: item.wait_send())
-    for h in range(2):
+    own_sends(lambda item: item.wait_send(), (whole,))
+    for h in (whole,):
         p = piece(z, ox, mine)
         to_y(p, h).wait_send()
         to_c(p, h).wait_send()
@@ -476,7 +491,7 @@
 
         @pl.when(zz >= 0 if way else zz < n_z)
         def _():
-            for h in range(2):
+            for h in (whole,):
                 p = piece(zz, x, mine)
 
                 @pl.when(z < n_z - 1 if way else z > 0)
@@ -584,11 +599,12 @@
             pltpu.VMEM((H_DEV, up), f32),
             dma((5,)),
             dma((3,)),
-            dma((2, n_scen * 4)),
-            dma((2, 2, n_scen * 4)),
-            dma((2, n_scen * 4)),
-            dma((2, n_scen * 4)),
-            dma((2, n_scen * 4)),
+            dma((2, n_scen * 2)),
+            dma((n_scen * 2,)),
+            dma((2, n_scen // 2)),
+            dma((n_scen,)),
+            dma((n_scen,)),
+            dma((n_scen * 2,)),
             dma((n_scen,)),
             dma((n_scen,)),
             dma((PASSES, 2)),

time: 50.9 us -> 46.2 us (0.908)
  Pallas kernels: 50 us -> 45.4 us
    pallas_call x1, Pallas kernels: 47.3 us -> 42.6 us  [fused(): pl.pallas_call(functools.partial(kernel, n_tm, n_scen, units), name='wind...]
where the time goes in v2:
time: 46.2 us; the launch traced here: 46 us
  Pallas kernels  45.4 us (98%)
  between operations  0.64 us (1%)
    pallas_call x1, Pallas kernels, fused(): pl.pallas_call(functools.partial(kernel, n_tm, n_scen, units), name='wind...  42.6 us
    pallas_call x1, Pallas kernels, fused(): pl.pallas_call(finish, name='finish', out_shape=shapes, in_specs=[vm] * 4...  2.72 us

profile of v2, /device:TPU:1, one launch (start us, length us, event | category | flops | bytes accessed | tf_op | source)
XLA Modules:
  0.0 46.0 jit_solution(18246049700075448311)
XLA Ops:
  0.6 42.6 %window.1 = (f32[600,256]{1,0:T(8,128)}, f32[600,256]{1,0:T(8,128)}, f32[600,256]{1,0:T(8,128)}, f32[8,600]{1,0:T(8,128)}) custom-call(bf16[320,2000]{1,0:T(8,128)(2,1)} %fl_hbm.1, f32[600,256]{1,0:T(8,128)} %pd_hbm.1, f32[600,256]{1,0:T(8,128)} %pc_hbm.1, f32[600,256]{1,0:T(8,128)} %mu_hbm.1, bf16[128,256]{1,0:T(8,128)(2,1)} %wind_hbm.1, s32[600]{0:T(1024)} %ub_ref.1, ...), custom_call_target="tpu_custom_call" | custom-call | tf_op jit(solution)/shard_map/window/pallas_call | solution.py:565
  43.3 2.7 %finish.1 = (f32[600,256]{1,0:T(8,128)}, f32[600,256]{1,0:T(8,128)}, f32[600,256]{1,0:T(8,128)}, f32[8,600]{1,0:T(8,128)}) custom-call(f32[600,256]{1,0:T(8,128)} %get-tuple-element.12.power_ref, f32[600,256]{1,0:T(8,128)} %get-tuple-element.13.commit_ref, f32[600,256]{1,0:T(8,128)} %get-tuple-element.14.mult_ref, f32[8,600]{1,0:T(8,128)} %get-tuple-element.15.cons_ref), custom_call_target="tpu_custom_call" | custom-call | tf_op jit(solution)/shard_map/finish/pallas_call | solution.py:619
